TPU v7x, 256 devices: a whole 4x4x8 slice. The times are simulated.
256 devices in a mesh: rows: 8 (over x, core), cols: 32 (over y, z).
Axes of the slice: x: 4, y: 4, z: 8, core: 2. Of those that a mesh axis runs over, the one named last changes fastest.
Arguments:
- features: bfloat16 [256, 4096, 1536], P('rows', 'cols'), may hold values from -6 to 6
- projection: bfloat16 [1536, 128], replicated, may hold values from -0.4375 to 0.4375
- prev_dist: float32 [256, 4096], P('rows', 'cols'), may hold values from 0.5 to 3
- valid: int32 [256, 4096], P('rows', 'cols'), may hold values 0 or 1
- pick_owner: int32 [512], replicated, may hold values from 0 to 255, as said below
- pick_slot: int32 [512], replicated, may hold values from 0 to 4095, as said below
Outputs:
- min_dist: float32 [256, 4096], P('rows', 'cols')
Inputs may be any that keep to these rules, and one draw needn't show every extreme that they name: `pick_owner`: no two picks name the same patch; picks fall on devices at random. `pick_slot`: see pick_owner.
All inputs are finite; a program needn't handle non-finite values. No bound on the sum of `valid` on one device may be relied on, other than what follows from the above.
Results may differ from a plain program's by a relative error of at most 0.0003.
Values may be sent and summed in bfloat16 or wider, within the bound.
A program may use at most 128 MiB of HBM per device.

v0:
```python
import jax
import jax.numpy as jnp
from jax import lax
from jax.sharding import PartitionSpec as P

D_PROJ = 128


def padded_2(block, sides, width):
    for axis, dim in sides:
        count = lax.axis_size(axis)
        forward = [(i, i + 1) for i in range(count - 1)]
        backward = [(target, source) for source, target in forward]
        low = lax.ppermute(
            lax.slice_in_dim(block, block.shape[dim] - width, None, axis=dim), axis, forward
        )
        high = lax.ppermute(lax.slice_in_dim(block, 0, width, axis=dim), axis, backward)
        block = jnp.concatenate([low, block, high], axis=dim)
    return block


def window_sum(padded, rows_dev, cols_dev):
    total = jnp.zeros((rows_dev, cols_dev, padded.shape[2]), jnp.float32)
    for row_off in range(3):
        for col_off in range(3):
            total = total + padded[
                row_off : row_off + rows_dev, col_off : col_off + cols_dev
            ].astype(jnp.float32)
    return total / 9.0


def shards(features, projection, prev_dist, valid, pick_owner, pick_slot):
    rows_dev, cols_dev, channels = features.shape
    proj_full = projection.astype(jnp.float32)
    own_index = lax.axis_index("rows") * lax.axis_size("cols") + lax.axis_index("cols")
    owned = pick_owner == own_index
    padded = padded_2(features, (("rows", 0), ("cols", 1)), 1)
    pooled = window_sum(padded, rows_dev, cols_dev).reshape(rows_dev * cols_dev, channels)
    projected = jnp.dot(pooled, proj_full, precision=lax.Precision.HIGHEST)
    local_rows = jnp.where(owned[:, None], projected[pick_slot], jnp.float32(0.0))
    pick_rows = lax.psum(local_rows, ("rows", "cols"))
    pick_sq = jnp.sum(pick_rows * pick_rows, axis=1)
    own_sq = jnp.sum(projected * projected, axis=1)
    inner_prod = jnp.dot(projected, pick_rows.T, precision=lax.Precision.HIGHEST)
    scaled_gap = (own_sq[:, None] + pick_sq[None, :] - 2.0 * inner_prod) / D_PROJ
    nearest = jnp.min(scaled_gap, axis=1).reshape(rows_dev, cols_dev)
    return jnp.where(valid == 1, jnp.minimum(prev_dist, nearest), jnp.float32(0.0))


def solution(mesh):
    return jax.shard_map(
        shards,
        mesh=mesh,
        in_specs=(P("rows", "cols", None), P(), P("rows", "cols"), P("rows", "cols"), P(), P()),
        out_specs=P("rows", "cols"),
        check_vma=False,
    )
```

profile of v0, /device:TPU:2, one launch (start us, length us, event | category | flops | bytes accessed | tf_op | source)
XLA Modules:
  0.0 382.1 jit_solution(17740806826330092399)
XLA Ops:
  6.5 0.0 copy-start
  6.5 0.0 all-reduce.2.cloned.1.call-start
  6.5 1.2 fusion.6
  7.8 1.9 collective-permute-start
  9.7 3.6 collective-permute-start.1
  13.3 0.7 broadcast_compare_fusion
  14.0 0.7 compare_select_fusion
  14.7 2.1 collective-permute-done
  16.9 6.7 %constant_dynamic-update-slice_fusion.1 = bf16[34,128,1536]{2,1,0:T(8,128)(2,1)S(1)} fusion(bf16[34,128,1536]{2,1,0:T(8,128)(2,1)S(1)} %constant_dynamic-update-slice_fusion.2, bf16[32,128,1536]{2,1,0:T(8,128)(2,1)} %param.6), kind=kLoop, calls=%fused_computation.25 | loop fusion | bytes 25165824
  23.6 0.0 collective-permute-done.1
  23.6 0.0 copy-start.1
  23.6 4.8 %copy-done.1 = bf16[34,128,1536]{2,1,0:T(8,128)(2,1)} copy-done((bf16[34,128,1536]{2,1,0:T(8,128)(2,1)}, bf16[34,128,1536]{2,1,0:T(8,128)(2,1)S(1)}, u32[]{:S(2)}) %copy-start.1) | copy-done | bytes 13369368
  28.5 0.3 fusion.5
  28.8 3.8 %collective-permute-start.2 = (bf16[34,1,1536]{2,0,1:T(8,128)(2,1)S(1)}, bf16[34,1,1536]{2,0,1:T(8,128)(2,1)S(1)}, u32[]{:S(2)}, u32[]{:S(2)}) collective-permute-start(bf16[34,1,1536]{2,0,1:T(8,128)(2,1)S(1)} %copy.15), channel_id=1, source_target_pairs={{0,1},{1,2},{2,3},{3,4},{4,5},{5,6},{6,7},{7,8},{8,9},{9,10},{10,1... | collective-permute-start | bytes 313352 | tf_op jit(solution)/shard_map/ppermute | solution.py:14
  32.7 1.3 collective-permute-start.3
  34.0 1.1 collective-permute-done.2
  35.1 0.2 copy.16
  35.2 4.2 %collective-permute-done.3 = bf16[34,1,1536]{2,0,1:T(8,128)(2,1)S(1)} collective-permute-done((bf16[34,1,1536]{2,0,1:T(8,128)(2,1)S(1)}, bf16[34,1,1536]{2,0,1:T(8,128)(2,1)S(1)}, u32[]{:S(2)}, u32[]{:S(2)}) %collective-permute-start.3) | collective-permute-done | bytes 104480 | tf_op jit(solution)/shard_map/ppermute | solution.py:17
  39.5 0.2 copy.18
  39.6 47.2 %add_multiply_fusion = f32[32,128,1536]{2,1,0:T(8,128)} fusion(bf16[32,128,1536]{2,1,0:T(8,128)(2,1)} %param.6, bf16[34,128,1536]{2,1,0:T(8,128)(2,1)} %copy-done.1, bf16[34,1,1536]{2,1,0:T(2,128)(2,1)S(1)} %copy.18, bf16[34,1,1536]{2,1,0:T(2,128)(2,1)S(1)} %copy.16, bf16[1,128,1536]{2,1,0:T(8,128)(2,1)S(1)} %collective-permute-done.1, ...), kind=kLoop, calls=%fused_computation.1 | loop fusion | flops 264241152 | bytes 52113408 | tf_op jit(solution)/shard_map/div | solution.py:29
  86.8 0.0 copy-done
  86.9 18.7 %multiply_reduce_fusion.1 = (f32[4096]{0:T(1024)S(1)}, f32[4096,128]{0,1:T(8,128)S(1)}) fusion(f32[4096,1536]{1,0:T(8,128)} %bitcast.9, bf16[1536,128]{1,0:T(8,128)(2,1)S(1)} %copy-done), kind=kOutput, calls=%fused_computation.19 | convolution fusion | flops 9664720896 | bytes 27672576 | tf_op jit(solution)/shard_map/dot_general | solution.py:39
  105.6 0.0 copy-start.2
  105.6 0.0 copy-start.3
  105.6 1.9 copy.19
  107.5 2.6 gather_fusion
  110.1 0.8 broadcast_select_fusion
  111.0 0.0 all-reduce.2.cloned.1.call-update
  111.0 253.3 %all-reduce.2.cloned.1.call-done = f32[512,128]{1,0:T(8,128)} async-done(((f32[512,128]{1,0:T(8,128)}), f32[512,128]{1,0:T(8,128)}) %all-reduce.2.cloned.1.call-update) | async-done | bytes 262160 | tf_op jit(solution)/shard_map/psum | solution.py:41
  364.3 1.1 multiply_reduce_fusion.2
  365.4 9.2 %multiply_reduce_fusion = f32[4096]{0:T(1024)S(1)} fusion(f32[4096,128]{0,1:T(8,128)S(1)} %get-tuple-element.10, f32[512,128]{1,0:T(8,128)} %all-reduce.2.cloned.1.call-done, f32[512]{0:T(512)S(1)} %multiply_reduce_fusion.2, f32[4096]{0:T(1024)S(1)} %get-tuple-element.9), kind=kOutput, calls=%fused_computation.18 | convolution fusion | flops 3231707136 | bytes 2394112 | tf_op jit(solution)/shard_map/dot_general | solution.py:44
  374.6 0.0 copy-done.2
  374.6 0.0 copy-done.3
  374.7 0.6 fusion.4
  (5 shorter events, 0.1 us)
Async XLA Ops:
  6.5 80.3 %copy-start = (bf16[1536,128]{1,0:T(8,128)(2,1)S(1)}, bf16[1536,128]{1,0:T(8,128)(2,1)}, u32[]{:S(2)}) copy-start(bf16[1536,128]{1,0:T(8,128)(2,1)} %param.7) | copy-start | bytes 1179652
  6.5 357.8 %all-reduce.2.cloned.1.call-start = ((), (), s32[]{:S(2)}) async-start(), calls=%async_computation | async-start | bytes 524288 | tf_op jit(solution)/shard_map/psum | solution.py:41
  7.8 9.1 %collective-permute-start = (bf16[1,128,1536]{2,1,0:T(8,128)(2,1)S(1)}, bf16[1,128,1536]{2,1,0:T(8,128)(2,1)S(1)}, u32[]{:S(2)}, u32[]{:S(2)}) collective-permute-start(bf16[1,128,1536]{2,1,0:T(8,128)(2,1)S(1)} %get-tuple-element.8), channel_id=1, source_target_pairs={{0,32},{32,64},{64,96},{96,128},{128,160},{160,192},{192,224},{1,3... | collective-permute-start | bytes 1179656 | tf_op jit(solution)/shard_map/ppermute | solution.py:14
  9.7 13.9 %collective-permute-start.1 = (bf16[1,128,1536]{2,1,0:T(8,128)(2,1)S(1)}, bf16[1,128,1536]{2,1,0:T(8,128)(2,1)S(1)}, u32[]{:S(2)}, u32[]{:S(2)}) collective-permute-start(bf16[1,128,1536]{2,1,0:T(8,128)(2,1)S(1)} %get-tuple-element.7), channel_id=1, source_target_pairs={{32,0},{64,32},{96,64},{128,96},{160,128},{192,160},{224,192},{33,... | collective-permute-start | bytes 1179656 | tf_op jit(solution)/shard_map/ppermute | solution.py:17
  23.6 4.8 %copy-start.1 = (bf16[34,128,1536]{2,1,0:T(8,128)(2,1)}, bf16[34,128,1536]{2,1,0:T(8,128)(2,1)S(1)}, u32[]{:S(2)}) copy-start(bf16[34,128,1536]{2,1,0:T(8,128)(2,1)S(1)} %constant_dynamic-update-slice_fusion) | copy-start | bytes 40108036
  28.8 6.3 %collective-permute-start.2 = (bf16[34,1,1536]{2,0,1:T(8,128)(2,1)S(1)}, bf16[34,1,1536]{2,0,1:T(8,128)(2,1)S(1)}, u32[]{:S(2)}, u32[]{:S(2)}) collective-permute-start(bf16[34,1,1536]{2,0,1:T(8,128)(2,1)S(1)} %copy.15), channel_id=1, source_target_pairs={{0,1},{1,2},{2,3},{3,4},{4,5},{5,6},{6,7},{7,8},{8,9},{9,10},{10,1... | collective-permute-start | bytes 313352 | tf_op jit(solution)/shard_map/ppermute | solution.py:14
  32.7 6.8 %collective-permute-start.3 = (bf16[34,1,1536]{2,0,1:T(8,128)(2,1)S(1)}, bf16[34,1,1536]{2,0,1:T(8,128)(2,1)S(1)}, u32[]{:S(2)}, u32[]{:S(2)}) collective-permute-start(bf16[34,1,1536]{2,0,1:T(8,128)(2,1)S(1)} %copy.17), channel_id=1, source_target_pairs={{1,0},{2,1},{3,2},{4,3},{5,4},{6,5},{7,6},{8,7},{9,8},{10,9},{11,1... | collective-permute-start | bytes 313352 | tf_op jit(solution)/shard_map/ppermute | solution.py:17
  105.6 269.0 %copy-start.2 = (f32[32,128]{1,0:T(8,128)S(1)}, f32[32,128]{1,0:T(8,128)}, u32[]{:S(2)}) copy-start(f32[32,128]{1,0:T(8,128)} %param.8) | copy-start | bytes 49156
  105.6 269.0 %copy-start.3 = (s32[32,128]{1,0:T(8,128)S(1)}, s32[32,128]{1,0:T(8,128)}, u32[]{:S(2)}) copy-start(s32[32,128]{1,0:T(8,128)} %param.9) | copy-start | bytes 49156
Sparse Core Ops, SparseCore 0:
  111.1 253.1 all-reduce.1
where the time goes:
time: 382 us
  waiting for transfers between devices  261 us (68%)
  other arithmetic  51.2 us (13%)
  matrix products  27.9 us (7%)
  local copies, waits for them, and re-layouts  18 us (5%)
  between operations  13.6 us (4%)
  starting transfers between devices  10.7 us (3%)
    psum x1, waiting for transfers between devices, shards(): pick_rows = lax.psum(local_rows, ('rows', 'cols'))  253 us
    div x1, other arithmetic, window_sum(): return total / 9.0  47.2 us
    dot_general x1, matrix products, shards(): projected = jnp.dot(pooled, proj_full, precision=lax.Precision.HIGHEST)  18.7 us
    unnamed x10, local copies, waits for them, and re-layouts  11.6 us
    dot_general x1, matrix products, shards(): jnp.dot(projected, pick_rows.T, precision=lax.Precision.HIGHEST)  9.21 us
  transfers between devices with their start and end apart: 5, of which 4 were waited for; matrix products, arithmetic and copies ran while one was open for 2% of the time, Pallas kernels for 0%

commit v1 on v0

--- a/solution.py
+++ b/solution.py
@@ -38,7 +38,7 @@
     pooled = window_sum(padded, rows_dev, cols_dev).reshape(rows_dev * cols_dev, channels)
     projected = jnp.dot(pooled, proj_full, precision=lax.Precision.HIGHEST)
     local_rows = jnp.where(owned[:, None], projected[pick_slot], jnp.float32(0.0))
-    pick_rows = lax.psum(local_rows, ("rows", "cols"))
+    pick_rows = lax.psum(lax.psum(local_rows, axis_name="cols"), axis_name="rows")
     pick_sq = jnp.sum(pick_rows * pick_rows, axis=1)
     own_sq = jnp.sum(projected * projected, axis=1)
     inner_prod = jnp.dot(projected, pick_rows.T, precision=lax.Precision.HIGHEST)

time: 382 us -> 340 us (0.89)
  waiting for transfers between devices: 261 us -> 216 us
    psum x1 -> x2, waiting for transfers between devices: 253 us -> 209 us  [the longest x1 147 us: shards(): lax.psum(local_rows, axis_name='cols')]
  transfers between devices with their start and end apart: 5 -> 6, of which waited for: 4 -> 5; matrix products, arithmetic and copies ran while one was open for 2% -> 2% of each run, Pallas kernels for 0% -> 0%
where the time goes in v1:
time: 340 us; the launch traced here: 338 us
  waiting for transfers between devices  216 us (64%)
  other arithmetic  51.2 us (15%)
  matrix products  27.8 us (8%)
  local copies, waits for them, and re-layouts  18 us (5%)
  between operations  13.6 us (4%)
  starting transfers between devices  10.9 us (3%)
    psum x1, waiting for transfers between devices, shards(): lax.psum(local_rows, axis_name='cols')  147 us
    psum x1, waiting for transfers between devices, shards(): lax.psum(lax.psum(local_rows, axis_name='cols'), axis_name='rows')  62 us
    div x1, other arithmetic, window_sum(): return total / 9.0  47.2 us
    dot_general x1, matrix products, shards(): projected = jnp.dot(pooled, proj_full, precision=lax.Precision.HIGHEST)  18.7 us
    unnamed x10, local copies, waits for them, and re-layouts  11.6 us
    dot_general x1, matrix products, shards(): jnp.dot(projected, pick_rows.T, precision=lax.Precision.HIGHEST)  9.02 us
  transfers between devices with their start and end apart: 6, of which 5 were waited for; matrix products, arithmetic and copies ran while one was open for 2% of the time, Pallas kernels for 0%

profile of v1, /device:TPU:2, one launch (start us, length us, event | category | flops | bytes accessed | tf_op | source)
XLA Modules:
  0.0 337.8 jit_solution(7706667509816880788)
XLA Ops:
  6.5 0.0 copy-start
  6.5 0.0 all-reduce.3.cloned.1.call-start
  6.5 1.2 fusion.6
  7.8 1.9 collective-permute-start
  9.7 3.6 %collective-permute-start.1 = (bf16[1,128,1536]{2,1,0:T(8,128)(2,1)S(1)}, bf16[1,128,1536]{2,1,0:T(8,128)(2,1)S(1)}, u32[]{:S(2)}, u32[]{:S(2)}) collective-permute-start(bf16[1,128,1536]{2,1,0:T(8,128)(2,1)S(1)} %get-tuple-element.7), channel_id=1, source_target_pairs={{32,0},{64,32},{96,64},{128,96},{160,128},{192,160},{224,192},{33,... | collective-permute-start | bytes 1179656 | tf_op jit(solution)/shard_map/ppermute | solution.py:17
  13.3 0.7 broadcast_compare_fusion
  14.0 0.7 compare_select_fusion
  14.7 2.1 collective-permute-done
  16.9 6.7 %constant_dynamic-update-slice_fusion.1 = bf16[34,128,1536]{2,1,0:T(8,128)(2,1)S(1)} fusion(bf16[34,128,1536]{2,1,0:T(8,128)(2,1)S(1)} %constant_dynamic-update-slice_fusion.2, bf16[32,128,1536]{2,1,0:T(8,128)(2,1)} %param.6), kind=kLoop, calls=%fused_computation.25 | loop fusion | bytes 25165824
  23.6 0.0 collective-permute-done.1
  23.6 0.0 copy-start.1
  23.6 4.8 %copy-done.1 = bf16[34,128,1536]{2,1,0:T(8,128)(2,1)} copy-done((bf16[34,128,1536]{2,1,0:T(8,128)(2,1)}, bf16[34,128,1536]{2,1,0:T(8,128)(2,1)S(1)}, u32[]{:S(2)}) %copy-start.1) | copy-done | bytes 13369368
  28.5 0.3 fusion.5
  28.8 3.8 %collective-permute-start.2 = (bf16[34,1,1536]{2,0,1:T(8,128)(2,1)S(1)}, bf16[34,1,1536]{2,0,1:T(8,128)(2,1)S(1)}, u32[]{:S(2)}, u32[]{:S(2)}) collective-permute-start(bf16[34,1,1536]{2,0,1:T(8,128)(2,1)S(1)} %copy.15), channel_id=1, source_target_pairs={{0,1},{1,2},{2,3},{3,4},{4,5},{5,6},{6,7},{7,8},{8,9},{9,10},{10,1... | collective-permute-start | bytes 313352 | tf_op jit(solution)/shard_map/ppermute | solution.py:14
  32.7 1.3 collective-permute-start.3
  34.0 1.1 collective-permute-done.2
  35.1 0.2 copy.16
  35.2 4.2 %collective-permute-done.3 = bf16[34,1,1536]{2,0,1:T(8,128)(2,1)S(1)} collective-permute-done((bf16[34,1,1536]{2,0,1:T(8,128)(2,1)S(1)}, bf16[34,1,1536]{2,0,1:T(8,128)(2,1)S(1)}, u32[]{:S(2)}, u32[]{:S(2)}) %collective-permute-start.3) | collective-permute-done | bytes 104480 | tf_op jit(solution)/shard_map/ppermute | solution.py:17
  39.5 0.2 copy.18
  39.6 47.2 %add_multiply_fusion = f32[32,128,1536]{2,1,0:T(8,128)} fusion(bf16[32,128,1536]{2,1,0:T(8,128)(2,1)} %param.6, bf16[34,128,1536]{2,1,0:T(8,128)(2,1)} %copy-done.1, bf16[34,1,1536]{2,1,0:T(2,128)(2,1)S(1)} %copy.18, bf16[34,1,1536]{2,1,0:T(2,128)(2,1)S(1)} %copy.16, bf16[1,128,1536]{2,1,0:T(8,128)(2,1)S(1)} %collective-permute-done.1, ...), kind=kLoop, calls=%fused_computation.1 | loop fusion | flops 264241152 | bytes 52113408 | tf_op jit(solution)/shard_map/div | solution.py:29
  86.9 0.0 copy-done
  86.9 18.7 %multiply_reduce_fusion.1 = (f32[4096]{0:T(1024)S(1)}, f32[4096,128]{0,1:T(8,128)S(1)}) fusion(f32[4096,1536]{1,0:T(8,128)} %bitcast.9, bf16[1536,128]{1,0:T(8,128)(2,1)S(1)} %copy-done), kind=kOutput, calls=%fused_computation.19 | convolution fusion | flops 9664720896 | bytes 27672576 | tf_op jit(solution)/shard_map/dot_general | solution.py:39
  105.6 0.0 copy-start.2
  105.6 0.0 copy-start.3
  105.6 1.9 copy.19
  107.5 2.6 gather_fusion
  110.1 0.8 broadcast_select_fusion
  111.0 0.0 all-reduce.3.cloned.1.call-update
  111.0 0.2 all-reduce.5.cloned.1.call-start
  111.2 146.9 %all-reduce.3.cloned.1.call-done = f32[512,128]{1,0:T(8,128)} async-done(((f32[512,128]{1,0:T(8,128)}), f32[512,128]{1,0:T(8,128)}) %all-reduce.3.cloned.1.call-update) | async-done | bytes 262160 | tf_op jit(solution)/shard_map/psum | solution.py:41
  258.1 0.0 all-reduce.5.cloned.1.call-update
  258.1 62.0 %all-reduce.5.cloned.1.call-done = f32[512,128]{1,0:T(8,128)} async-done(((f32[512,128]{1,0:T(8,128)}), f32[512,128]{1,0:T(8,128)}) %all-reduce.5.cloned.1.call-update) | async-done | bytes 262160 | tf_op jit(solution)/shard_map/psum | solution.py:41
  320.2 1.1 multiply_reduce_fusion.2
  321.3 9.0 %multiply_reduce_fusion = f32[4096]{0:T(1024)S(1)} fusion(f32[4096,128]{0,1:T(8,128)S(1)} %get-tuple-element.10, f32[512,128]{1,0:T(8,128)} %all-reduce.5.cloned.1.call-done, f32[512]{0:T(512)S(1)} %multiply_reduce_fusion.2, f32[4096]{0:T(1024)S(1)} %get-tuple-element.9), kind=kOutput, calls=%fused_computation.18 | convolution fusion | flops 3231707136 | bytes 2394112 | tf_op jit(solution)/shard_map/dot_general | solution.py:44
  330.3 0.0 copy-done.2
  330.3 0.0 copy-done.3
  330.3 0.6 fusion.4
  (5 shorter events, 0.1 us)
Async XLA Ops:
  6.5 80.3 %copy-start = (bf16[1536,128]{1,0:T(8,128)(2,1)S(1)}, bf16[1536,128]{1,0:T(8,128)(2,1)}, u32[]{:S(2)}) copy-start(bf16[1536,128]{1,0:T(8,128)(2,1)} %param.7) | copy-start | bytes 1179652
  6.5 251.6 %all-reduce.3.cloned.1.call-start = ((), (), s32[]{:S(2)}) async-start(), calls=%async_computation | async-start | bytes 524288 | tf_op jit(solution)/shard_map/psum | solution.py:41
  7.8 9.1 %collective-permute-start = (bf16[1,128,1536]{2,1,0:T(8,128)(2,1)S(1)}, bf16[1,128,1536]{2,1,0:T(8,128)(2,1)S(1)}, u32[]{:S(2)}, u32[]{:S(2)}) collective-permute-start(bf16[1,128,1536]{2,1,0:T(8,128)(2,1)S(1)} %get-tuple-element.8), channel_id=1, source_target_pairs={{0,32},{32,64},{64,96},{96,128},{128,160},{160,192},{192,224},{1,3... | collective-permute-start | bytes 1179656 | tf_op jit(solution)/shard_map/ppermute | solution.py:14
  9.7 13.9 %collective-permute-start.1 = (bf16[1,128,1536]{2,1,0:T(8,128)(2,1)S(1)}, bf16[1,128,1536]{2,1,0:T(8,128)(2,1)S(1)}, u32[]{:S(2)}, u32[]{:S(2)}) collective-permute-start(bf16[1,128,1536]{2,1,0:T(8,128)(2,1)S(1)} %get-tuple-element.7), channel_id=1, source_target_pairs={{32,0},{64,32},{96,64},{128,96},{160,128},{192,160},{224,192},{33,... | collective-permute-start | bytes 1179656 | tf_op jit(solution)/shard_map/ppermute | solution.py:17
  23.6 4.8 %copy-start.1 = (bf16[34,128,1536]{2,1,0:T(8,128)(2,1)}, bf16[34,128,1536]{2,1,0:T(8,128)(2,1)S(1)}, u32[]{:S(2)}) copy-start(bf16[34,128,1536]{2,1,0:T(8,128)(2,1)S(1)} %constant_dynamic-update-slice_fusion) | copy-start | bytes 40108036
  28.8 6.3 %collective-permute-start.2 = (bf16[34,1,1536]{2,0,1:T(8,128)(2,1)S(1)}, bf16[34,1,1536]{2,0,1:T(8,128)(2,1)S(1)}, u32[]{:S(2)}, u32[]{:S(2)}) collective-permute-start(bf16[34,1,1536]{2,0,1:T(8,128)(2,1)S(1)} %copy.15), channel_id=1, source_target_pairs={{0,1},{1,2},{2,3},{3,4},{4,5},{5,6},{6,7},{7,8},{8,9},{9,10},{10,1... | collective-permute-start | bytes 313352 | tf_op jit(solution)/shard_map/ppermute | solution.py:14
  32.7 6.8 %collective-permute-start.3 = (bf16[34,1,1536]{2,0,1:T(8,128)(2,1)S(1)}, bf16[34,1,1536]{2,0,1:T(8,128)(2,1)S(1)}, u32[]{:S(2)}, u32[]{:S(2)}) collective-permute-start(bf16[34,1,1536]{2,0,1:T(8,128)(2,1)S(1)} %copy.17), channel_id=1, source_target_pairs={{1,0},{2,1},{3,2},{4,3},{5,4},{6,5},{7,6},{8,7},{9,8},{10,9},{11,1... | collective-permute-start | bytes 313352 | tf_op jit(solution)/shard_map/ppermute | solution.py:17
  105.6 224.7 %copy-start.2 = (f32[32,128]{1,0:T(8,128)S(1)}, f32[32,128]{1,0:T(8,128)}, u32[]{:S(2)}) copy-start(f32[32,128]{1,0:T(8,128)} %param.8) | copy-start | bytes 49156
  105.6 224.7 %copy-start.3 = (s32[32,128]{1,0:T(8,128)S(1)}, s32[32,128]{1,0:T(8,128)}, u32[]{:S(2)}) copy-start(s32[32,128]{1,0:T(8,128)} %param.9) | copy-start | bytes 49156
  111.0 209.2 %all-reduce.5.cloned.1.call-start = ((), (), s32[]{:S(2)}) async-start(), calls=%async_computation.1 | async-start | bytes 524288 | tf_op jit(solution)/shard_map/psum | solution.py:41
Sparse Core Ops, SparseCore 0:
  111.1 146.9 all-reduce.2
  260.4 59.6 all-reduce.4
